TPU v7x, 32 devices: a whole 2x2x4 slice. The times are simulated.
32 devices in a mesh: groups: 2 (over x), seq: 16 (over z, y, core).
Axes of the slice: x: 2, y: 2, z: 4, core: 2. Of those that a mesh axis runs over, the one named last changes fastest.
Arguments:
- video: bfloat16 [32, 256, 1152], P(('groups', 'seq')), parts along dimension 0, may hold values from -6 to 6
- spatial_qkv: bfloat16 [1152, 3456], P(None, 'seq'), may hold values from -0.53033009 to 0.53033009
- spatial_out: bfloat16 [1152, 1152], P(None, 'seq'), may hold values from -0.1875 to 0.1875
- temporal_qkv: bfloat16 [1152, 3456], P(None, 'seq'), may hold values from -0.53033009 to 0.53033009
- temporal_out: bfloat16 [1152, 1152], P(None, 'seq'), may hold values from -0.1875 to 0.1875
Outputs:
- video_out: bfloat16 [32, 256, 1152], P(('groups', 'seq')), parts along dimension 0
There are 2 independent parts, one for each index of `groups`. A program takes and returns all parts, laid end to end along the dimension named above; an argument that names none is the same for every part. Nothing has to cross between parts.
All inputs are finite; a program needn't handle non-finite values.
Results may differ from a plain program's by a relative error of at most 0.023.
The roundings to bfloat16 on the way count: a program that leaves them out, or rounds other values in their place, can miss the bound.
Values may be sent and summed in bfloat16 or wider, within the bound.
A program may use at most 128 MiB of HBM per device.

v0:
```python
import math

import jax
import jax.numpy as jnp
from jax import lax
from jax.sharding import PartitionSpec as P

HEADS = 16


epsilon = 1e-06


def normalize(values):
    average = jnp.mean(values, axis=-1, keepdims=True)
    centered = values - average
    spread = jnp.mean(centered * centered, axis=-1, keepdims=True)
    return (centered * lax.rsqrt(spread + epsilon)).astype(jnp.bfloat16)


def split_heads(table, leading, second, which):
    width = table.shape[1] // 3
    block = table[:, which * width : (which + 1) * width]
    return block.reshape(leading, second, HEADS, width // HEADS)


def attend(queries, key_rows, value_rows, score_form, mix_form):
    head_width = queries.shape[-1]

    def one_head(parts):
        head_query, head_key, head_value = parts
        scores = jnp.einsum(
            score_form, head_query, head_key, preferred_element_type=jnp.float32
        ) / math.sqrt(head_width)
        highest = jnp.max(scores, axis=-1, keepdims=True)
        powers = jnp.exp(scores - highest)
        probs = (powers / jnp.sum(powers, axis=-1, keepdims=True)).astype(jnp.bfloat16)
        return jnp.einsum(mix_form, probs, head_value, preferred_element_type=jnp.float32).astype(
            jnp.bfloat16
        )

    stacked = lax.map(
        one_head,
        (jnp.moveaxis(queries, 2, 0), jnp.moveaxis(key_rows, 2, 0), jnp.moveaxis(value_rows, 2, 0)),
    )
    moved = jnp.moveaxis(stacked, 0, 2)
    return moved.reshape(moved.shape[0], moved.shape[1], -1)


def temporal_block(tokens, project_qkv, project_out):
    frames, count, width = tokens.shape
    rows = tokens.reshape(frames * count, width)
    table = project_qkv(normalize(rows.astype(jnp.float32)))
    mixed = attend(
        split_heads(table, frames, count, 0),
        split_heads(table, frames, count, 1),
        split_heads(table, frames, count, 2),
        "fpe,gpe->pfg",
        "pfg,gpe->fpe",
    )
    update = project_out(mixed.reshape(frames * count, width))
    return (rows.astype(jnp.float32) + update).astype(jnp.bfloat16).reshape(frames, count, width)


def local(video, spatial_qkv, spatial_out, temporal_qkv, temporal_out):
    frames_here, patches, width = video.shape
    devices_seq = lax.axis_size("seq")
    rows = video.reshape(frames_here * patches, width)
    normed = normalize(rows.astype(jnp.float32))
    table = jnp.dot(
        normed,
        lax.all_gather(spatial_qkv, "seq", axis=1, tiled=True),
        preferred_element_type=jnp.float32,
    ).astype(jnp.bfloat16)
    mixed = attend(
        split_heads(table, frames_here, patches, 0),
        split_heads(table, frames_here, patches, 1),
        split_heads(table, frames_here, patches, 2),
        "fpe,fqe->fpq",
        "fpq,fqe->fpe",
    )
    mixed_rows = mixed.reshape(frames_here * patches, width)
    update = jnp.dot(
        mixed_rows,
        lax.all_gather(spatial_out, "seq", axis=1, tiled=True),
        preferred_element_type=jnp.float32,
    )
    hidden = (rows.astype(jnp.float32) + update).astype(jnp.bfloat16)
    blocks = hidden.reshape(frames_here, devices_seq, patches // devices_seq, width)
    received = lax.all_to_all(blocks, "seq", split_axis=1, concat_axis=0, tiled=True)

    def gathered_qkv(normed_rows):
        return jnp.dot(
            normed_rows,
            lax.all_gather(temporal_qkv, "seq", axis=1, tiled=True),
            preferred_element_type=jnp.float32,
        ).astype(jnp.bfloat16)

    def gathered_out(mixed_block):
        return jnp.dot(
            mixed_block,
            lax.all_gather(temporal_out, "seq", axis=1, tiled=True),
            preferred_element_type=jnp.float32,
        )

    frames, single, count, width_in = received.shape
    result = temporal_block(received.reshape(frames, count, width_in), gathered_qkv, gathered_out)
    positioned = result.reshape(frames, single, count, width_in)
    returned = lax.all_to_all(positioned, "seq", split_axis=0, concat_axis=1, tiled=True)
    return returned.reshape(frames_here, patches, width)


def solution(mesh):
    placed = (
        P(("groups", "seq"), None, None),
        P(None, "seq"),
        P(None, "seq"),
        P(None, "seq"),
        P(None, "seq"),
    )
    return jax.shard_map(
        local,
        mesh=mesh,
        in_specs=placed,
        out_specs=P(("groups", "seq"), None, None),
        check_vma=False,
    )
```

profile of v0, /device:TPU:0, one launch (start us, length us, event | category | flops | bytes accessed | tf_op | source)
XLA Modules:
  0.0 299.7 jit_solution(7854589238866505058)
XLA Ops:
  6.5 0.7 all-gather.5.cloned.1.call-update
  7.3 0.7 all-gather.7.cloned.1.call-update
  8.1 0.7 all-gather.9.cloned.1.call-update
  8.9 0.3 fusion.57
  9.2 75.2 %all-gather.5.cloned.1.call-done = bf16[1152,3456]{0,1:T(8,128)(2,1)} async-done(((bf16[1152,216]{0,1:T(8,128)(2,1)}), bf16[1152,3456]{0,1:T(8,128)(2,1)}) %all-gather.5.cloned.1.call-update) | async-done | bytes 7962640 | tf_op jit(solution)/shard_map/all_gather | solution.py:72
  84.5 5.9 %convolution_convert_fusion.3 = bf16[256,3456]{1,0:T(8,128)(2,1)S(1)} fusion(bf16[1152,3456]{0,1:T(8,128)(2,1)} %all-gather.5.cloned.1.call-done, bf16[1,256,1152]{2,1,0:T(8,128)(2,1)S(1)} %copy-done.1, f32[256]{0:T(256)S(1)} %add_rsqrt_fusion.1, f32[256]{0:T(256)S(1)} %broadcast_multiply_fusion.1), kind=kOutput, calls=%fused_computation.40 | convolution fusion | flops 2040496128 | bytes 10323968 | tf_op jit(solution)/shard_map/dot_general | solution.py:70
  91.2 8.1 %while.20 = (s32[]{:T(128)}, bf16[16,1,256,72]{2,3,1,0:T(8,128)(2,1)S(1)}, bf16[16,1,256,72]{2,3,0,1:T(8,128)(2,1)S(1)}, bf16[16,1,256,72]{2,3,0,1:T(8,128)(2,1)...) while((s32[]{:T(128)}, bf16[16,1,256,72]{2,3,1,0:T(8,128)(2,1)S(1)}, ...), condition=%wide.region_5.6_spmd, body=%wide.region_2.5_spmd.sunk | while | flops 19351040 | bytes 941125 | solution.py:42
  92.3 0.3 fusion.91
  93.8 0.3 fusion.91
  94.8 0.3 fusion.91
  97.3 0.3 fusion.91
  98.9 0.3 fusion.91
  99.4 29.0 %all-gather.7.cloned.1.call-done = bf16[1152,1152]{0,1:T(8,128)(2,1)} async-done(((bf16[1152,72]{0,1:T(8,128)(2,1)}), bf16[1152,1152]{0,1:T(8,128)(2,1)}) %all-gather.7.cloned.1.call-update) | async-done | bytes 2654224 | tf_op jit(solution)/shard_map/all_gather | solution.py:85
  128.4 3.6 %fusion.52 = bf16[256,1152]{1,0:T(8,128)(2,1)} fusion(bf16[256,1152]{0,1:T(8,128)(2,1)S(1)} %bitcast.141, bf16[1152,1152]{0,1:T(8,128)(2,1)} %all-gather.7.cloned.1.call-done, bf16[1,256,1152]{2,1,0:T(8,128)(2,1)S(1)} %copy-done.1), kind=kOutput, calls=%fused_computation.43 | convolution fusion | flops 680361984 | bytes 4423680 | tf_op jit(solution)/shard_map/dot_general | solution.py:83
  132.0 3.6 %all-to-all-start = ((bf16[1,16,16,1152]{3,2,0,1:T(8,128)(2,1)}), bf16[1,16,16,1152]{3,2,0,1:T(8,128)(2,1)S(1)}, u32[]{:S(2)}, u32[]{:S(2)}) async-start(bf16[1,16,16,1152]{3,2,0,1:T(8,128)(2,1)} %bitcast.19), calls=%async_computation | async-start | bytes 1179648 | tf_op jit(solution)/shard_map/all_to_all | solution.py:90
  135.8 0.3 all-gather.11.cloned.1.call-update
  136.1 23.1 %all-to-all-done = bf16[1,16,16,1152]{3,2,0,1:T(8,128)(2,1)S(1)} async-done(((bf16[1,16,16,1152]{3,2,0,1:T(8,128)(2,1)}), bf16[1,16,16,1152]{3,2,0,1:T(8,128)(2,1)S(1)}, u32[]{:S(2)}, u32[]{:S(2)}) %all-to-all-start) | async-done | bytes 589856 | tf_op jit(solution)/shard_map/all_to_all | solution.py:90
  159.5 0.3 multiply_reduce_fusion
  159.9 0.3 fusion.60
  160.2 52.2 %all-gather.9.cloned.1.call-done = bf16[1152,3456]{0,1:T(8,128)(2,1)} async-done(((bf16[1152,216]{0,1:T(8,128)(2,1)}), bf16[1152,3456]{0,1:T(8,128)(2,1)}) %all-gather.9.cloned.1.call-update) | async-done | bytes 7962640 | tf_op jit(solution)/shard_map/all_gather | solution.py:95
  212.3 5.8 %convolution_convert_fusion.2 = bf16[256,3456]{1,0:T(8,128)(2,1)S(1)} fusion(bf16[256,1152]{1,0:T(8,128)(2,1)S(1)} %fusion.60, bf16[1152,3456]{0,1:T(8,128)(2,1)} %all-gather.9.cloned.1.call-done), kind=kOutput, calls=%fused_computation.39 | convolution fusion | flops 2039316480 | bytes 10321920 | tf_op jit(solution)/shard_map/dot_general | solution.py:93
  218.3 1.8 reshape.132
  220.1 2.9 reshape.133
  223.0 1.8 reshape.131
  224.8 1.7 copy.44
  226.5 2.7 copy_bitcast_fusion
  229.2 38.3 %while.21 = (s32[]{:T(128)}, bf16[16,16,16,72]{3,1,2,0:T(8,128)(2,1)S(1)}, bf16[16,16,16,72]{3,1,2,0:T(8,128)(2,1)}, bf16[16,16,16,72]{3,1,2,0:T(8,128)(2,1)}, bf16[16,16,16,72]{3,1,2,0:T(8,128)(2,1)}, /*index=5*/s32[]{:T(128)}) while((s32[]{:T(128)}, bf16[16,16,16,72]{3,1,2,0:T(8,128)(2,1)S(1)}, bf16[16,16,16,72]{3,1,2,0:T(8,128)(2,1)}, ...), condition=%wide.region_11.12_spmd, body=%wide.region_8.11_spmd.sunk | while | flops 1816864 | bytes 405573 | solution.py:42
  229.2 1.1 fusion.99
  230.3 1.3 fusion.100
  231.6 1.1 fusion.99
  232.7 1.3 fusion.100
  234.0 1.1 fusion.99
  235.1 1.3 fusion.100
  236.4 1.1 fusion.99
  237.4 1.4 fusion.100
  238.8 1.1 fusion.99
  239.9 1.3 fusion.100
  241.2 1.1 fusion.99
  242.3 1.3 fusion.100
  243.6 1.1 fusion.99
  244.7 1.3 fusion.100
  246.0 1.1 fusion.99
  247.1 1.3 fusion.100
  248.4 1.1 fusion.99
  249.5 1.3 fusion.100
  250.8 1.1 fusion.99
  251.8 1.3 fusion.100
  253.1 1.1 fusion.99
  254.2 1.3 fusion.100
  255.6 1.1 fusion.99
  256.6 1.3 fusion.100
  257.9 1.1 fusion.99
  259.0 1.3 fusion.100
  260.3 1.1 fusion.99
  261.4 1.3 fusion.100
  262.7 1.1 fusion.99
  263.8 1.3 fusion.100
  265.1 1.1 fusion.99
  266.2 1.3 fusion.100
  267.5 0.7 copy.35
  268.2 1.3 reshape_reshape.11
  269.5 2.8 fusion.53
  272.2 20.1 %all_to_all.8 = bf16[16,1,16,1152]{3,2,1,0:T(8,128)(2,1)S(1)} all-to-all(bf16[16,1,16,1152]{3,2,1,0:T(8,128)(2,1)S(1)} %bitcast.140), channel_id=1, replica_groups=mesh['groups'=2,'seq'=16] {'seq'}, dimensions={0} | all-to-all | bytes 1179648 | tf_op jit(solution)/shard_map/all_to_all | solution.py:109
  292.3 0.8 copy.62
  (69 shorter events, 8.6 us)
Async XLA Ops:
  6.5 2.2 copy-start.1
  6.5 77.9 %all-gather.5.cloned.1.call-start = ((), (), s32[]{:S(2)}) async-start(), calls=%async_computation.2 | async-start | bytes 8460288 | tf_op jit(solution)/shard_map/all_gather | solution.py:72
  7.3 121.1 %all-gather.7.cloned.1.call-start = ((), (), s32[]{:S(2)}) async-start(), calls=%async_computation.3 | async-start | bytes 2820096 | tf_op jit(solution)/shard_map/all_gather | solution.py:85
  8.0 204.3 %all-gather.9.cloned.1.call-start = ((), (), s32[]{:S(2)}) async-start(), calls=%async_computation.4 | async-start | bytes 8460288 | tf_op jit(solution)/shard_map/all_gather | solution.py:95
  132.0 27.3 %all-to-all-start = ((bf16[1,16,16,1152]{3,2,0,1:T(8,128)(2,1)}), bf16[1,16,16,1152]{3,2,0,1:T(8,128)(2,1)S(1)}, u32[]{:S(2)}, u32[]{:S(2)}) async-start(bf16[1,16,16,1152]{3,2,0,1:T(8,128)(2,1)} %bitcast.19), calls=%async_computation | async-start | bytes 1179648 | tf_op jit(solution)/shard_map/all_to_all | solution.py:90
  135.6 133.9 %all-gather.11.cloned.1.call-start = ((), (), s32[]{:S(2)}) async-start(), calls=%async_computation.5 | async-start | bytes 2820096 | tf_op jit(solution)/shard_map/all_gather | solution.py:102
  224.8 1.7 copy-start
  226.5 2.7 copy-start.2
Sparse Core Ops, SparseCore 0:
  9.5 74.8 all-gather.4
  86.6 41.7 all-gather.6
  130.5 81.7 all-gather.8
  214.3 41.6 all-gather.10
where the time goes:
time: 302 us; the launch traced here: 300 us
  waiting for transfers between devices  182 us (60%)
  matrix products  62.9 us (21%)
  blocking collectives  20.1 us (7%)
  local copies, waits for them, and re-layouts  14.8 us (5%)
  between operations  13.3 us (4%)
  starting transfers between devices  3.88 us (1%)
    all_gather x1, waiting for transfers between devices, local(): lax.all_gather(spatial_qkv, 'seq', axis=1, tiled=True)  75.2 us
    all_gather x1, waiting for transfers between devices, gathered_qkv(): lax.all_gather(temporal_qkv, 'seq', axis=1, tiled=True)  52.2 us
    all_gather x1, waiting for transfers between devices, local(): lax.all_gather(spatial_out, 'seq', axis=1, tiled=True)  29 us
    dot_general x32, matrix products, one_head(): jnp.einsum(mix_form, probs, head_value, preferred_element_type=jnp.float32)  23.4 us
    all_to_all x1, waiting for transfers between devices, local(): lax.all_to_all(blocks, 'seq', split_axis=1, concat_axis=0, tiled=True)  23.1 us
    all_to_all x1, blocking collectives, local(): lax.all_to_all(positioned, 'seq', split_axis=0, concat_axis=1, tiled=True)  20.1 us
    sub x16, matrix products, one_head(): powers = jnp.exp(scores - highest)  17.2 us
    reshape x4, local copies, waits for them, and re-layouts, split_heads(): return block.reshape(leading, second, HEADS, width // HEADS)  8.18 us
  transfers between devices with their start and end apart: 5, of which 4 were waited for; matrix products, arithmetic and copies ran while one was open for 26% of the time, Pallas kernels for 0%

commit v1 on v0

v1 whole, which is shorter than its diff:
```python
import functools
import math

import jax
import jax.numpy as jnp
from jax import lax
from jax.experimental import pallas as pl
from jax.experimental.pallas import tpu as pltpu
from jax.sharding import PartitionSpec as P

HEADS = 16
epsilon = 1e-06
MESH = pl.DeviceIdType.MESH


def normalize_into(x_ref, xt_ref, nt_ref):
    xt_ref[...] = x_ref[...].astype(jnp.float32).T
    values = xt_ref[...]
    centered = values - jnp.mean(values, axis=0, keepdims=True)
    spread = jnp.mean(centered * centered, axis=0, keepdims=True)
    nt_ref[...] = (centered * lax.rsqrt(spread + epsilon)).astype(jnp.bfloat16)


def project_shard(w_ref, shard, nt_ref, table_ref):
    blocks, rows, width = w_ref.shape[1:]
    head = table_ref.shape[1]
    out = jnp.dot(
        w_ref[shard].reshape(blocks * rows, width), nt_ref[...], preferred_element_type=jnp.float32
    ).astype(jnp.bfloat16)
    for j in range(blocks):
        table_ref[shard * blocks + j] = out[j * rows : j * rows + head]


def attend_pair(pair, table_ref, mixed_ref, same):
    head = table_ref.shape[1]
    parts = []
    for j in range(2):
        h = pair * 2 + j
        q, k, v = table_ref[h], table_ref[HEADS + h], table_ref[2 * HEADS + h]
        scores = lax.dot_general(
            k, q, (((0,), (0,)), ((), ())), preferred_element_type=jnp.float32
        ) * (1.0 / math.sqrt(head))
        if same is not None:
            scores = jnp.where(same(scores.shape), scores, -jnp.inf)
        powers = jnp.exp(scores - jnp.max(scores, axis=0, keepdims=True))
        total = jnp.sum(powers, axis=0, keepdims=True)
        probs = (powers * (1.0 / total)).astype(jnp.bfloat16)
        parts.append(jnp.dot(v, probs, preferred_element_type=jnp.float32))
    both = jnp.concatenate(parts, axis=0).astype(jnp.bfloat16)
    mixed_ref[pl.ds(pl.multiple_of(pair * 2 * head, 16), 2 * head), :] = both


def project_out(w_ref, mixed_ref, xt_ref, out_ref, head):
    shards, blocks, rows, width = w_ref.shape
    low = head // 16 * 16
    step = 4

    @pl.loop(0, shards // step)
    def _(i):
        weights = w_ref[pl.ds(i * step, step), :, low:, :].reshape(-1, width)
        update = jnp.dot(weights, mixed_ref[...], preferred_element_type=jnp.float32)
        update = update.reshape(step * blocks, rows - low, -1)[:, head - low :]
        count = step * blocks * (rows - head)
        at = pl.ds(pl.multiple_of(i * count, 8), count)
        xt_ref[at, :] = xt_ref[at, :] + update.reshape(count, -1)

    out_ref[...] = xt_ref[...].T.astype(jnp.bfloat16)


def same_by(kind, size):
    def same(shape):
        a = lax.broadcasted_iota(jnp.int32, shape, 0)
        b = lax.broadcasted_iota(jnp.int32, shape, 1)
        return (a % size == b % size) if kind == "mod" else (a // size == b // size)

    return same


def sublayer_kernel(same, x_ref, w_ref, out_ref, xt_ref, nt_ref, table_ref, mixed_ref):
    normalize_into(x_ref, xt_ref, nt_ref)

    @pl.loop(0, w_ref.shape[0])
    def _(d):
        project_shard(w_ref, d, nt_ref, table_ref)

    @pl.loop(0, HEADS // 2)
    def _(pair):
        attend_pair(pair, table_ref, mixed_ref, same)

    project_out(w_ref, mixed_ref, xt_ref, out_ref, table_ref.shape[1])


def compute_scratch(tokens, width):
    return [
        pltpu.VMEM((width, tokens), jnp.float32),
        pltpu.VMEM((width, tokens), jnp.bfloat16),
        pltpu.VMEM((3 * HEADS, width // HEADS, tokens), jnp.bfloat16),
        pltpu.VMEM((width, tokens), jnp.bfloat16),
    ]


def sublayer(x, w, same):
    tokens, width = x.shape
    return pl.pallas_call(
        functools.partial(sublayer_kernel, same),
        out_shape=jax.ShapeDtypeStruct(x.shape, jnp.bfloat16),
        in_specs=[pl.BlockSpec(memory_space=pltpu.VMEM)] * 2,
        out_specs=pl.BlockSpec(memory_space=pltpu.VMEM),
        scratch_shapes=compute_scratch(tokens, width),
        compiler_params=pltpu.CompilerParams(vmem_limit_bytes=40 << 20),
    )(x, w)


def blocks_of(qkv, out, count):
    width = qkv.shape[0]
    return jnp.concatenate(
        [qkv.T.reshape(count, -1, width), out.T.reshape(count, -1, width)], axis=1
    )


def gathered(qkv, out):
    if lax.axis_size("seq") == HEADS:
        return lax.all_gather(blocks_of(qkv, out, 3), "seq", axis=0)
    full = blocks_of(
        lax.all_gather(qkv, "seq", axis=1, tiled=True),
        lax.all_gather(out, "seq", axis=1, tiled=True),
        3 * HEADS,
    )
    return full.reshape(HEADS, 3, *full.shape[1:])


def plain(video, spatial_qkv, spatial_out, temporal_qkv, temporal_out):
    frames_here, patches, width = video.shape
    n = lax.axis_size("seq")
    count = patches // n
    same_s = None if frames_here == 1 else same_by("div", patches)
    hidden = sublayer(video.reshape(-1, width), gathered(spatial_qkv, spatial_out), same_s)
    blocks = hidden.reshape(frames_here, n, count, width)
    received = lax.all_to_all(blocks, "seq", split_axis=1, concat_axis=0, tiled=True)
    result = sublayer(
        received.reshape(-1, width), gathered(temporal_qkv, temporal_out), same_by("mod", count)
    )
    positioned = result.reshape(frames_here * n, 1, count, width)
    returned = lax.all_to_all(positioned, "seq", split_axis=0, concat_axis=1, tiled=True)
    return returned.reshape(frames_here, patches, width)


def solution(mesh):
    split = P(None, "seq")
    placed = (P(("groups", "seq"), None, None), split, split, split, split)
    return jax.shard_map(
        plain,
        mesh=mesh,
        in_specs=placed,
        out_specs=placed[0],
        check_vma=False,
    )
```

time: 302 us -> 247 us (0.82)
  the two profiles are of different devices: /device:TPU:0 before, /device:TPU:29 now
where the time goes in v1:
time: 247 us; the launch traced here: 242 us
  waiting for transfers between devices  160 us (65%)
  Pallas kernels  30.3 us (12%)
  blocking collectives  19.9 us (8%)
  between operations  13.4 us (5%)
  local copies, waits for them, and re-layouts  8.86 us (4%)
  starting transfers between devices  6.57 us (3%)
  other arithmetic  3.01 us (1%)
    all_gather x2, waiting for transfers between devices, gathered(): return lax.all_gather(blocks_of(qkv, out, 3), 'seq', axis=0)  160 us
    pallas_call x2, Pallas kernels, sublayer(): pl.pallas_call(functools.partial(sublayer_kernel, same), out_shape=jax.Sh...  30.3 us
    all_to_all x1, blocking collectives, plain(): lax.all_to_all(positioned, 'seq', split_axis=0, concat_axis=1, tiled=True)  19.9 us
    unnamed x11, local copies, waits for them, and re-layouts  8.86 us
    all_to_all x1, starting transfers between devices, plain(): lax.all_to_all(blocks, 'seq', split_axis=1, concat_axis=0, tiled=True)  6.53 us
  transfers between devices with their start and end apart: 3, of which 2 were waited for; matrix products, arithmetic and copies ran while one was open for 0% of the time, Pallas kernels for 6%

profile of v1, /device:TPU:29, one launch (start us, length us, event | category | flops | bytes accessed | tf_op | source)
XLA Modules:
  0.0 242.3 jit_solution(1154720030236003413)
XLA Ops:
  6.5 0.0 copy-start.4
  6.5 0.0 copy-start.3
  6.5 0.0 all-gather.5.cloned.1.call-start
  6.5 2.1 pad_maximum_fusion
  8.6 0.0 copy-start.2
  8.6 0.0 all-gather.5.cloned.1.call-update
  8.7 0.0 all-gather.7.cloned.1.call-start
  8.7 0.0 copy-done.4
  8.7 0.0 copy-done.3
  8.7 0.9 pad_maximum_fusion.1
  9.7 0.0 all-gather.7.cloned.1.call-update
  9.7 87.3 %all-gather.5.cloned.1.call-done = bf16[48,96,1152]{2,1,0:T(8,128)(2,1)} async-done(((bf16[3,96,1152]{2,1,0:T(8,128)(2,1)}), bf16[48,96,1152]{2,1,0:T(8,128)(2,1)}) %all-gather.5.cloned.1.call-update) | async-done | bytes 10616848 | tf_op jit(solution)/shard_map/all_gather | solution.py:123
  97.0 0.0 copy-done.2
  97.0 0.0 copy-start.1
  97.0 4.0 %copy-done.1 = bf16[48,96,1152]{2,1,0:T(8,128)(2,1)S(1)} copy-done((bf16[48,96,1152]{2,1,0:T(8,128)(2,1)S(1)}, bf16[48,96,1152]{2,1,0:T(8,128)(2,1)}, u32[]{:S(2)}) %copy-start.1) | copy-done | bytes 10616856
  101.0 15.6 %shard_map.55 = bf16[256,1152]{1,0:T(8,128)(2,1)} custom-call(bf16[256,1152]{1,0:T(8,128)(2,1)S(1)} %bitcast.27, bf16[16,3,96,1152]{3,2,1,0:T(8,128)(2,1)S(1)} %bitcast.24), custom_call_target="tpu_custom_call" | custom-call | tf_op jit(solution)/shard_map/pallas_call | solution.py:104
  116.6 6.5 %all-to-all-start = ((bf16[1,16,16,1152]{3,2,0,1:T(8,128)(2,1)}), bf16[1,16,16,1152]{3,2,0,1:T(8,128)(2,1)S(1)}, u32[]{:S(2)}, u32[]{:S(2)}) async-start(bf16[1,16,16,1152]{3,2,0,1:T(8,128)(2,1)} %bitcast.7), calls=%async_computation | async-start | bytes 1179648 | tf_op jit(solution)/shard_map/all_to_all | solution.py:139
  123.1 72.8 %all-gather.7.cloned.1.call-done = bf16[48,96,1152]{2,1,0:T(8,128)(2,1)} async-done(((bf16[3,96,1152]{2,1,0:T(8,128)(2,1)}), bf16[48,96,1152]{2,1,0:T(8,128)(2,1)}) %all-gather.7.cloned.1.call-update) | async-done | bytes 10616848 | tf_op jit(solution)/shard_map/all_gather | solution.py:123
  195.9 0.0 all-to-all-done
  195.9 0.0 copy-start
  195.9 4.0 %copy-done = bf16[48,96,1152]{2,1,0:T(8,128)(2,1)S(1)} copy-done((bf16[48,96,1152]{2,1,0:T(8,128)(2,1)S(1)}, bf16[48,96,1152]{2,1,0:T(8,128)(2,1)}, u32[]{:S(2)}) %copy-start) | copy-done | bytes 10616856
  200.0 14.7 %shard_map.56 = bf16[256,1152]{1,0:T(8,128)(2,1)S(1)} custom-call(bf16[256,1152]{1,0:T(8,128)(2,1)S(1)} %bitcast.25, bf16[16,3,96,1152]{3,2,1,0:T(8,128)(2,1)S(1)} %bitcast.23), custom_call_target="tpu_custom_call" | custom-call | tf_op jit(solution)/shard_map/pallas_call | solution.py:104
  214.7 19.9 %all_to_all.8 = bf16[16,1,16,1152]{3,2,1,0:T(8,128)(2,1)S(1)} all-to-all(bf16[16,1,16,1152]{3,2,1,0:T(8,128)(2,1)S(1)} %bitcast.26), channel_id=1, replica_groups=mesh['groups'=2,'seq'=16] {'seq'}, dimensions={0} | all-to-all | bytes 1179648 | tf_op jit(solution)/shard_map/all_to_all | solution.py:144
  234.6 0.8 copy.9
Async XLA Ops:
  6.5 2.2 copy-start.4
  6.5 2.2 copy-start.3
  6.5 90.5 %all-gather.5.cloned.1.call-start = ((), (), s32[]{:S(2)}) async-start(), calls=%async_computation.2 | async-start | bytes 11280384 | tf_op jit(solution)/shard_map/all_gather | solution.py:123
  8.6 88.4 %copy-start.2 = (bf16[1,256,1152]{2,1,0:T(8,128)(2,1)S(1)}, bf16[1,256,1152]{2,1,0:T(8,128)(2,1)}, u32[]{:S(2)}) copy-start(bf16[1,256,1152]{2,1,0:T(8,128)(2,1)} %param.5) | copy-start | bytes 1769476
  8.7 187.3 %all-gather.7.cloned.1.call-start = ((), (), s32[]{:S(2)}) async-start(), calls=%async_computation.3 | async-start | bytes 11280384 | tf_op jit(solution)/shard_map/all_gather | solution.py:123
  97.0 4.0 %copy-start.1 = (bf16[48,96,1152]{2,1,0:T(8,128)(2,1)S(1)}, bf16[48,96,1152]{2,1,0:T(8,128)(2,1)}, u32[]{:S(2)}) copy-start(bf16[48,96,1152]{2,1,0:T(8,128)(2,1)} %all-gather.5.cloned.1.call-done) | copy-start | bytes 31850500
  116.6 79.3 %all-to-all-start = ((bf16[1,16,16,1152]{3,2,0,1:T(8,128)(2,1)}), bf16[1,16,16,1152]{3,2,0,1:T(8,128)(2,1)S(1)}, u32[]{:S(2)}, u32[]{:S(2)}) async-start(bf16[1,16,16,1152]{3,2,0,1:T(8,128)(2,1)} %bitcast.7), calls=%async_computation | async-start | bytes 1179648 | tf_op jit(solution)/shard_map/all_to_all | solution.py:139
  195.9 4.0 %copy-start = (bf16[48,96,1152]{2,1,0:T(8,128)(2,1)S(1)}, bf16[48,96,1152]{2,1,0:T(8,128)(2,1)}, u32[]{:S(2)}) copy-start(bf16[48,96,1152]{2,1,0:T(8,128)(2,1)} %all-gather.7.cloned.1.call-done) | copy-start | bytes 31850500
Sparse Core Ops, SparseCore 0:
  9.6 87.3 all-gather.4
  99.3 96.5 all-gather.6

commit v2 on v1

--- a/solution.py
+++ b/solution.py
@@ -145,11 +145,229 @@
     return returned.reshape(frames_here, patches, width)
 
 
+def ring_position(chip, chips):
+    odd = lax.rem(chip, 2)
+    return (1 - odd) * lax.div(chip, 2) + odd * (chips - 1 - lax.div(chip, 2))
+
+
+def ring_chip(position, chips):
+    back = lax.div(position, chips // 2)
+    return (1 - back) * 2 * position + back * (2 * (chips - 1 - position) + 1)
+
+
+def fused_kernel(
+    n, groups, count, x_ref, ws_ref, wt_ref, out_ref,
+    w_ref, xt_ref, nt_ref, table_ref, mixed_ref, sent_ref, got_ref,
+    land_sem, ring_sem, other_sem, sib_sem, go_sem, come_sem,
+):
+    chips = n // 2
+    half = chips // 2
+    me = lax.axis_index("seq")
+    group = lax.axis_index("groups")
+    core = lax.rem(me, 2)
+    sibling = me + 1 - 2 * core
+    side = lax.rem(group, 2)
+    other = group + 1 - 2 * side
+    place = ring_position(lax.div(me, 2), chips)
+    by_ring, by_other = 2 * side, 2 - 2 * side
+
+    def device(offset, which):
+        return 2 * ring_chip(lax.rem(place + offset + chips, chips), chips) + which
+
+    ahead = (device(1, core), device(-1, core))
+
+    barrier = pltpu.get_barrier_semaphore()
+    for j in range(1, n):
+        pl.semaphore_signal(
+            barrier, inc=1, device_id={"seq": lax.rem(me + j, n)}, device_id_type=MESH
+        )
+    pl.semaphore_signal(barrier, inc=1, device_id={"groups": other}, device_id_type=MESH)
+    pl.semaphore_wait(barrier, n)
+
+    sends = []
+
+    def copy(phase, shard, piece, send_sem, target):
+        return pltpu.make_async_remote_copy(
+            src_ref=w_ref.at[phase, shard, piece],
+            dst_ref=w_ref.at[phase, shard, piece],
+            send_sem=send_sem.at[phase, shard, piece],
+            recv_sem=land_sem.at[phase, shard, piece],
+            device_id=target,
+            device_id_type=MESH,
+        )
+
+    def send(*what):
+        one = copy(*what)
+        one.start()
+        sends.append(one)
+
+    def along(phase, shard, piece, way):
+        send(phase, shard, piece, ring_sem.at[way], {"seq": ahead[way]})
+
+    def beside(phase, shard, piece):
+        send(phase, shard, piece, sib_sem, {"seq": sibling})
+
+    def across(phase, shard):
+        send(phase, shard, by_ring, other_sem, {"groups": other})
+
+    def landed(phase, shard, piece):
+        copy(phase, shard, piece, sib_sem, {"seq": sibling}).wait_recv()
+
+    reach = ((by_ring, (half - 1, half)), (1, (half, half - 1)))
+
+    def start(phase):
+        for piece, far in reach:
+            for way in range(2):
+                along(phase, me, piece, way)
+        for piece in range(3):
+            beside(phase, me, piece)
+
+    def step(phase, s):
+        for piece, far in reach:
+            for way in range(2):
+                if s <= far[way]:
+                    shard = device(-s if way == 0 else s, core)
+                    landed(phase, shard, piece)
+                    if s < far[way]:
+                        along(phase, shard, piece, way)
+                    if piece is by_ring:
+                        across(phase, shard)
+                    beside(phase, shard, piece)
+
+    def offsets(s):
+        return (0,) if s == 0 else (s,) if s == half else (-s, s)
+
+    def from_other(phase, s):
+        for offset in offsets(s):
+            shard = device(offset, core)
+            landed(phase, shard, by_other)
+            beside(phase, shard, by_other)
+
+    def from_sibling(phase, s):
+        for offset in offsets(s):
+            for piece in range(3):
+                landed(phase, device(offset, 1 - core), piece)
+
+    def project(phase, s, which):
+        for offset in offsets(s):
+            project_shard(w_ref.at[phase], device(offset, which), nt_ref, table_ref)
+
+    def rows(index):
+        return pl.ds(pl.multiple_of(index * count, count), count)
+
+    def swap(phase, away, home):
+        return pltpu.make_async_remote_copy(
+            src_ref=sent_ref.at[phase, rows(away), :],
+            dst_ref=got_ref.at[phase, rows(home), :],
+            send_sem=go_sem.at[phase, away],
+            recv_sem=come_sem.at[phase, home],
+            device_id={"seq": away},
+            device_id_type=MESH,
+        )
+
+    def exchange(phase):
+        for j in range(1, n):
+            one = swap(phase, lax.rem(me + j, n), me)
+            one.start()
+            sends.append(one)
+        got_ref[phase, rows(me), :] = sent_ref[phase, rows(me), :]
+
+    def exchanged(phase):
+        for j in range(1, n):
+            peer = lax.rem(me + j, n)
+            swap(phase, peer, peer).wait_recv()
+
+    def attend(low, high, same):
+        @pl.loop(low, high)
+        def _(pair):
+            attend_pair(pair, table_ref, mixed_ref, same)
+
+    head = table_ref.shape[1]
+    pairs = HEADS // 2
+
+    w_ref[0, me] = ws_ref[...]
+    start(0)
+    w_ref[1, me] = wt_ref[...]
+    normalize_into(x_ref, xt_ref, nt_ref)
+    project(0, 0, core)
+    for s in range(1, half + 1):
+        step(0, s)
+        if s == half - 1:
+            start(1)
+        if s > 1:
+            from_other(0, s - 1)
+            project(0, s - 1, core)
+        from_sibling(0, max(s - 2, 0)) if s != 2 else None
+        project(0, max(s - 2, 0), 1 - core) if s != 2 else None
+    from_other(0, half)
+    project(0, half, core)
+    step(1, 1)
+    for s in range(half - 1, half + 1):
+        from_sibling(0, s)
+        project(0, s, 1 - core)
+    attend(0, pairs, None)
+    step(1, 2)
+    project_out(w_ref.at[0], mixed_ref, xt_ref, sent_ref.at[0], head)
+    exchange(0)
+    from_other(1, 1)
+    for s in range(3, half + 1):
+        step(1, s)
+        from_other(1, s - 1)
+    exchanged(0)
+    normalize_into(got_ref.at[0], xt_ref, nt_ref)
+    project(1, 0, core)
+    from_sibling(1, 0)
+    project(1, 0, 1 - core)
+    from_other(1, half)
+    for s in range(1, half + 1):
+        project(1, s, core)
+    for s in range(1, half + 1):
+        from_sibling(1, s)
+        project(1, s, 1 - core)
+    attend(0, pairs, same_by("mod", count))
+    project_out(w_ref.at[1], mixed_ref, xt_ref, sent_ref.at[1], head)
+    exchange(1)
+    exchanged(1)
+    out_ref[...] = got_ref[1]
+    for one in sends:
+        one.wait_send()
+
+
+def fused(video, spatial_qkv, spatial_out, temporal_qkv, temporal_out):
+    _, patches, width = video.shape
+    n, groups = lax.axis_size("seq"), lax.axis_size("groups")
+    ws = blocks_of(spatial_qkv, spatial_out, 3)
+    wt = blocks_of(temporal_qkv, temporal_out, 3)
+    dma = pltpu.SemaphoreType.DMA
+    out = pl.pallas_call(
+        functools.partial(fused_kernel, n, groups, patches // n),
+        out_shape=jax.ShapeDtypeStruct((patches, width), jnp.bfloat16),
+        in_specs=[pl.BlockSpec(memory_space=pltpu.VMEM)] * 3,
+        out_specs=pl.BlockSpec(memory_space=pltpu.VMEM),
+        scratch_shapes=[pltpu.VMEM((2, n, *ws.shape), jnp.bfloat16)]
+        + compute_scratch(patches, width)
+        + [pltpu.VMEM((2, patches, width), jnp.bfloat16)] * 2
+        + [dma((2, n, 3)), dma((2, 2, n, 3)), dma((2, n, 3)), dma((2, n, 3))]
+        + [dma((2, n)), dma((2, n))],
+        compiler_params=pltpu.CompilerParams(
+            collective_id=0, has_side_effects=True, vmem_limit_bytes=56 << 20
+        ),
+    )(video.reshape(patches, width), ws, wt)
+    return out.reshape(video.shape)
+
+
+def local(video, spatial_qkv, *rest):
+    n, groups = lax.axis_size("seq"), lax.axis_size("groups")
+    frames_here, patches, _ = video.shape
+    ringed = n == HEADS and groups % 2 == 0 and frames_here == 1 and patches % (16 * n) == 0
+    return (fused if ringed else plain)(video, spatial_qkv, *rest)
+
+
 def solution(mesh):
     split = P(None, "seq")
     placed = (P(("groups", "seq"), None, None), split, split, split, split)
     return jax.shard_map(
-        plain,
+        local,
         mesh=mesh,
         in_specs=placed,
         out_specs=placed[0],

time: 247 us -> 126 us (0.51); the launches traced: 242 us -> 126 us
  waiting for transfers between devices: 160 us -> 0 us
  Pallas kernels: 30.3 us -> 121 us
  blocking collectives: 19.9 us -> 0 us
  between operations: 13.4 us -> 0.01 us
  local copies, waits for them, and re-layouts: 8.86 us -> 1.92 us
  starting transfers between devices: 6.57 us -> 0 us
    all_gather x2 -> x0, waiting for transfers between devices: 160 us -> none  [gathered(): return lax.all_gather(blocks_of(qkv, out, 3), 'seq', axis=0)]
    pallas_call x2 -> x1, Pallas kernels: 30.3 us -> 121 us  [fused(): pl.pallas_call(functools.partial(fused_kernel, n, groups, patches // n),...]
    all_to_all x1 -> x0, blocking collectives: 19.9 us -> none  [plain(): lax.all_to_all(positioned, 'seq', split_axis=0, concat_axis=1, tiled=True)]
    unnamed x11 -> x1, local copies, waits for them, and re-layouts: 8.86 us -> 1.92 us
    all_to_all x1 -> x0, starting transfers between devices: 6.53 us -> none  [plain(): lax.all_to_all(blocks, 'seq', split_axis=1, concat_axis=0, tiled=True)]
  transfers between devices with their start and end apart: 3 -> 0, of which waited for: 2 -> 0; matrix products, arithmetic and copies ran while one was open for 0% -> 0% of each run, Pallas kernels for 6% -> 0%
where the time goes in v2:
time: 126 us
  Pallas kernels  121 us (96%)
  other arithmetic  2.49 us (2%)
  local copies, waits for them, and re-layouts  1.92 us (2%)
    pallas_call x1, Pallas kernels, fused(): pl.pallas_call(functools.partial(fused_kernel, n, groups, patches // n),...  121 us

profile of v2, /device:TPU:29, one launch (start us, length us, event | category | flops | bytes accessed | tf_op | source)
XLA Modules:
  0.0 125.6 jit_solution(4674330227539019509)
XLA Ops:
  0.0 2.5 %pad_maximum_fusion = (bf16[3,96,1152]{2,1,0:T(8,128)(2,1)}, bf16[3,96,1152]{2,1,0:T(8,128)(2,1)}) fusion(bf16[3,24,1152]{2,1,0:T(8,128)(2,1)} %bitcast.18, bf16[3,72,1152]{2,1,0:T(8,128)(2,1)} %bitcast.16, bf16[3,24,1152]{2,1,0:T(8,128)(2,1)} %bitcast.19, bf16[3,72,1152]{2,1,0:T(8,128)(2,1)} %bitcast.17), kind=kLoop, calls=%fused_computation | loop fusion | flops 2654208 | bytes 2654208 | tf_op jit(solution)/shard_map/concatenate | solution.py:116
  2.5 121.1 %shard_map.55 = bf16[256,1152]{1,0:T(8,128)(2,1)} custom-call(bf16[256,1152]{1,0:T(8,128)(2,1)} %bitcast.15, bf16[3,96,1152]{2,1,0:T(8,128)(2,1)} %get-tuple-element.5.ws_ref, bf16[3,96,1152]{2,1,0:T(8,128)(2,1)} %get-tuple-element.6.wt_ref), custom_call_target="tpu_custom_call" | custom-call | tf_op jit(solution)/shard_map/pallas_call | solution.py:342
  123.6 1.9 %copy.7 = bf16[1,256,1152]{2,1,0:T(8,128)(2,1)} copy(bf16[1,256,1152]{2,1,0:T(8,128)(2,1)} %bitcast.14) | data formatting | bytes 1179648

commit v3 on v2

--- a/solution.py
+++ b/solution.py
@@ -31,12 +31,12 @@
         table_ref[shard * blocks + j] = out[j * rows : j * rows + head]
 
 
-def attend_pair(pair, table_ref, mixed_ref, same):
+def attend_pair(pair, table_ref, mixed_ref, same, low=0, high=None):
     head = table_ref.shape[1]
     parts = []
     for j in range(2):
         h = pair * 2 + j
-        q, k, v = table_ref[h], table_ref[HEADS + h], table_ref[2 * HEADS + h]
+        q, k, v = table_ref[h, :, low:high], table_ref[HEADS + h], table_ref[2 * HEADS + h]
         scores = lax.dot_general(
             k, q, (((0,), (0,)), ((), ())), preferred_element_type=jnp.float32
         ) * (1.0 / math.sqrt(head))
@@ -47,24 +47,25 @@
         probs = (powers * (1.0 / total)).astype(jnp.bfloat16)
         parts.append(jnp.dot(v, probs, preferred_element_type=jnp.float32))
     both = jnp.concatenate(parts, axis=0).astype(jnp.bfloat16)
-    mixed_ref[pl.ds(pl.multiple_of(pair * 2 * head, 16), 2 * head), :] = both
-
-
-def project_out(w_ref, mixed_ref, xt_ref, out_ref, head):
+    mixed_ref[pl.ds(pl.multiple_of(pair * 2 * head, 16), 2 * head), low:high] = both
+
+
+def project_out(w_ref, mixed_ref, xt_ref, out_ref, head, first=0, last=None):
     shards, blocks, rows, width = w_ref.shape
     low = head // 16 * 16
     step = 4
+    tokens = slice(first, last)
 
     @pl.loop(0, shards // step)
     def _(i):
         weights = w_ref[pl.ds(i * step, step), :, low:, :].reshape(-1, width)
-        update = jnp.dot(weights, mixed_ref[...], preferred_element_type=jnp.float32)
+        update = jnp.dot(weights, mixed_ref[:, tokens], preferred_element_type=jnp.float32)
         update = update.reshape(step * blocks, rows - low, -1)[:, head - low :]
         count = step * blocks * (rows - head)
         at = pl.ds(pl.multiple_of(i * count, 8), count)
-        xt_ref[at, :] = xt_ref[at, :] + update.reshape(count, -1)
-
-    out_ref[...] = xt_ref[...].T.astype(jnp.bfloat16)
+        xt_ref[at, tokens] = xt_ref[at, tokens] + update.reshape(count, -1)
+
+    out_ref[tokens, :] = xt_ref[:, tokens].T.astype(jnp.bfloat16)
 
 
 def same_by(kind, size):
@@ -204,14 +205,26 @@
     def along(phase, shard, piece, way):
         send(phase, shard, piece, ring_sem.at[way], {"seq": ahead[way]})
 
-    def beside(phase, shard, piece):
-        send(phase, shard, piece, sib_sem, {"seq": sibling})
+    def whole(phase, shard):
+        return pltpu.make_async_remote_copy(
+            src_ref=w_ref.at[phase, shard],
+            dst_ref=w_ref.at[phase, shard],
+            send_sem=sib_sem.at[phase, shard],
+            recv_sem=land_sem.at[phase, shard, 0],
+            device_id={"seq": sibling},
+            device_id_type=MESH,
+        )
+
+    def beside(phase, shard):
+        one = whole(phase, shard)
+        one.start()
+        sends.append(one)
 
     def across(phase, shard):
         send(phase, shard, by_ring, other_sem, {"groups": other})
 
     def landed(phase, shard, piece):
-        copy(phase, shard, piece, sib_sem, {"seq": sibling}).wait_recv()
+        copy(phase, shard, piece, other_sem, {"groups": other}).wait_recv()
 
     reach = ((by_ring, (half - 1, half)), (1, (half, half - 1)))
 
@@ -219,8 +232,7 @@
         for piece, far in reach:
             for way in range(2):
                 along(phase, me, piece, way)
-        for piece in range(3):
-            beside(phase, me, piece)
+        beside(phase, me)
 
     def step(phase, s):
         for piece, far in reach:
@@ -232,7 +244,6 @@
                         along(phase, shard, piece, way)
                     if piece is by_ring:
                         across(phase, shard)
-                    beside(phase, shard, piece)
 
     def offsets(s):
         return (0,) if s == 0 else (s,) if s == half else (-s, s)
@@ -241,12 +252,11 @@
         for offset in offsets(s):
             shard = device(offset, core)
             landed(phase, shard, by_other)
-            beside(phase, shard, by_other)
+            beside(phase, shard)
 
     def from_sibling(phase, s):
         for offset in offsets(s):
-            for piece in range(3):
-                landed(phase, device(offset, 1 - core), piece)
+            whole(phase, device(offset, 1 - core)).wait_recv()
 
     def project(phase, s, which):
         for offset in offsets(s):
@@ -255,32 +265,49 @@
     def rows(index):
         return pl.ds(pl.multiple_of(index * count, count), count)
 
+    def slot(index):
+        return lax.rem(index, 2) * chips + lax.div(index, 2)
+
     def swap(phase, away, home):
+        leaving = rows(away if phase == 0 else slot(away))
+        landing = rows(slot(home) if phase == 0 else home)
         return pltpu.make_async_remote_copy(
-            src_ref=sent_ref.at[phase, rows(away), :],
-            dst_ref=got_ref.at[phase, rows(home), :],
+            src_ref=sent_ref.at[phase, leaving, :],
+            dst_ref=got_ref.at[phase, landing, :],
             send_sem=go_sem.at[phase, away],
             recv_sem=come_sem.at[phase, home],
             device_id={"seq": away},
             device_id_type=MESH,
         )
 
-    def exchange(phase):
+    def exchange(phase, start=True):
         for j in range(1, n):
             one = swap(phase, lax.rem(me + j, n), me)
-            one.start()
+            if start:
+                one.start()
             sends.append(one)
-        got_ref[phase, rows(me), :] = sent_ref[phase, rows(me), :]
+
+    def exchange_half(which):
+        for j in range(chips):
+            away = 2 * lax.rem(lax.div(me, 2) + j, chips) + which
+            if j == 0:
+
+                @pl.when(core != which)
+                def _():
+                    swap(1, away, me).start()
+
+            else:
+                swap(1, away, me).start()
 
     def exchanged(phase):
         for j in range(1, n):
             peer = lax.rem(me + j, n)
             swap(phase, peer, peer).wait_recv()
 
-    def attend(low, high, same):
+    def attend(low, high, same, *tokens):
         @pl.loop(low, high)
         def _(pair):
-            attend_pair(pair, table_ref, mixed_ref, same)
+            attend_pair(pair, table_ref, mixed_ref, same, *tokens)
 
     head = table_ref.shape[1]
     pairs = HEADS // 2
@@ -309,6 +336,7 @@
     step(1, 2)
     project_out(w_ref.at[0], mixed_ref, xt_ref, sent_ref.at[0], head)
     exchange(0)
+    got_ref[0, rows(slot(me)), :] = sent_ref[0, rows(me), :]
     from_other(1, 1)
     for s in range(3, half + 1):
         step(1, s)
@@ -318,15 +346,20 @@
     project(1, 0, core)
     from_sibling(1, 0)
     project(1, 0, 1 - core)
+    for s in range(1, half):
+        project(1, s, core)
     from_other(1, half)
-    for s in range(1, half + 1):
-        project(1, s, core)
+    project(1, half, core)
     for s in range(1, half + 1):
         from_sibling(1, s)
         project(1, s, 1 - core)
-    attend(0, pairs, same_by("mod", count))
-    project_out(w_ref.at[1], mixed_ref, xt_ref, sent_ref.at[1], head)
-    exchange(1)
+    for which in range(2):
+        tokens = (which * chips * count, (which + 1) * chips * count)
+        attend(0, pairs, same_by("mod", count), *tokens)
+        project_out(w_ref.at[1], mixed_ref, xt_ref, sent_ref.at[1], head, *tokens)
+        exchange_half(which)
+    exchange(1, start=False)
+    got_ref[1, rows(me), :] = sent_ref[1, rows(slot(me)), :]
     exchanged(1)
     out_ref[...] = got_ref[1]
     for one in sends:
@@ -347,7 +380,7 @@
         scratch_shapes=[pltpu.VMEM((2, n, *ws.shape), jnp.bfloat16)]
         + compute_scratch(patches, width)
         + [pltpu.VMEM((2, patches, width), jnp.bfloat16)] * 2
-        + [dma((2, n, 3)), dma((2, 2, n, 3)), dma((2, n, 3)), dma((2, n, 3))]
+        + [dma((2, n, 3)), dma((2, 2, n, 3)), dma((2, n, 3)), dma((2, n))]
         + [dma((2, n)), dma((2, n))],
         compiler_params=pltpu.CompilerParams(
             collective_id=0, has_side_effects=True, vmem_limit_bytes=56 << 20

time: 126 us -> 125 us (level)
  no operation moved by 1% of the time
where the time goes in v3:
time: 125 us
  Pallas kernels  121 us (97%)
  other arithmetic  2.49 us (2%)
  local copies, waits for them, and re-layouts  1.92 us (2%)
    pallas_call x1, Pallas kernels, fused(): pl.pallas_call(functools.partial(fused_kernel, n, groups, patches // n),...  121 us

profile of v3, /device:TPU:29, one launch (start us, length us, event | category | flops | bytes accessed | tf_op | source)
XLA Modules:
  0.0 125.0 jit_solution(16817053797281591954)
XLA Ops:
  0.0 2.5 %pad_maximum_fusion = (bf16[3,96,1152]{2,1,0:T(8,128)(2,1)}, bf16[3,96,1152]{2,1,0:T(8,128)(2,1)}) fusion(bf16[3,24,1152]{2,1,0:T(8,128)(2,1)} %bitcast.18, bf16[3,72,1152]{2,1,0:T(8,128)(2,1)} %bitcast.16, bf16[3,24,1152]{2,1,0:T(8,128)(2,1)} %bitcast.19, bf16[3,72,1152]{2,1,0:T(8,128)(2,1)} %bitcast.17), kind=kLoop, calls=%fused_computation | loop fusion | flops 2654208 | bytes 2654208 | tf_op jit(solution)/shard_map/concatenate | solution.py:117
  2.5 120.6 %shard_map.55 = bf16[256,1152]{1,0:T(8,128)(2,1)} custom-call(bf16[256,1152]{1,0:T(8,128)(2,1)} %bitcast.15, bf16[3,96,1152]{2,1,0:T(8,128)(2,1)} %get-tuple-element.5.ws_ref, bf16[3,96,1152]{2,1,0:T(8,128)(2,1)} %get-tuple-element.6.wt_ref), custom_call_target="tpu_custom_call" | custom-call | tf_op jit(solution)/shard_map/pallas_call | solution.py:375
  123.1 1.9 %copy.7 = bf16[1,256,1152]{2,1,0:T(8,128)(2,1)} copy(bf16[1,256,1152]{2,1,0:T(8,128)(2,1)} %bitcast.14) | data formatting | bytes 1179648

commit v4 on v3

--- a/solution.py
+++ b/solution.py
@@ -281,7 +281,7 @@
         )
 
     def exchange(phase, start=True):
-        for j in range(1, n):
+        for j in sorted(range(1, n), key=lambda i: -min(i, n - i)):
             one = swap(phase, lax.rem(me + j, n), me)
             if start:
                 one.start()
@@ -324,14 +324,13 @@
         if s > 1:
             from_other(0, s - 1)
             project(0, s - 1, core)
-        from_sibling(0, max(s - 2, 0)) if s != 2 else None
-        project(0, max(s - 2, 0), 1 - core) if s != 2 else None
+        from_sibling(0, s - 1)
+        project(0, s - 1, 1 - core)
     from_other(0, half)
     project(0, half, core)
     step(1, 1)
-    for s in range(half - 1, half + 1):
-        from_sibling(0, s)
-        project(0, s, 1 - core)
+    from_sibling(0, half)
+    project(0, half, 1 - core)
     attend(0, pairs, None)
     step(1, 2)
     project_out(w_ref.at[0], mixed_ref, xt_ref, sent_ref.at[0], head)

time: 125 us -> 125 us (level)
  no operation moved by 1% of the time
where the time goes in v4:
time: 125 us
  Pallas kernels  120 us (96%)
  other arithmetic  2.49 us (2%)
  local copies, waits for them, and re-layouts  1.92 us (2%)
    pallas_call x1, Pallas kernels, fused(): pl.pallas_call(functools.partial(fused_kernel, n, groups, patches // n),...  120 us

profile of v4, /device:TPU:29, one launch (start us, length us, event | category | flops | bytes accessed | tf_op | source)
XLA Modules:
  0.0 124.6 jit_solution(5606346437231518284)
XLA Ops:
  0.0 2.5 %pad_maximum_fusion = (bf16[3,96,1152]{2,1,0:T(8,128)(2,1)}, bf16[3,96,1152]{2,1,0:T(8,128)(2,1)}) fusion(bf16[3,24,1152]{2,1,0:T(8,128)(2,1)} %bitcast.18, bf16[3,72,1152]{2,1,0:T(8,128)(2,1)} %bitcast.16, bf16[3,24,1152]{2,1,0:T(8,128)(2,1)} %bitcast.19, bf16[3,72,1152]{2,1,0:T(8,128)(2,1)} %bitcast.17), kind=kLoop, calls=%fused_computation | loop fusion | flops 2654208 | bytes 2654208 | tf_op jit(solution)/shard_map/concatenate | solution.py:117
  2.5 120.2 %shard_map.55 = bf16[256,1152]{1,0:T(8,128)(2,1)} custom-call(bf16[256,1152]{1,0:T(8,128)(2,1)} %bitcast.15, bf16[3,96,1152]{2,1,0:T(8,128)(2,1)} %get-tuple-element.5.ws_ref, bf16[3,96,1152]{2,1,0:T(8,128)(2,1)} %get-tuple-element.6.wt_ref), custom_call_target="tpu_custom_call" | custom-call | tf_op jit(solution)/shard_map/pallas_call | solution.py:374
  122.7 1.9 %copy.7 = bf16[1,256,1152]{2,1,0:T(8,128)(2,1)} copy(bf16[1,256,1152]{2,1,0:T(8,128)(2,1)} %bitcast.14) | data formatting | bytes 1179648
